TPU v7x, 32 devices: a whole 2x2x4 slice. The times are simulated.
32 devices in a mesh: pipe: 2 (over y), ctx: 4 (over x, core), dp: 4 (over z).
Axes of the slice: x: 2, y: 2, z: 4, core: 2. Of those that a mesh axis runs over, the one named last changes fastest.
Arguments:
- hidden_in: bfloat16 [2, 4, 2048, 3584], P('pipe', 'dp', 'ctx'), may hold values from -6 to 6
- selected: int32 [2, 4, 32, 16], P('pipe', 'dp', 'ctx'), may hold values from -1 to 31, as said below
- norm_gain: float32 [2, 3584], P('pipe'), may hold values from 0.1 to 1.9
- kv_weight: bfloat16 [2, 3584, 512], P('pipe', ('ctx', 'dp')), may hold values from -0.1875 to 0.1875
- gate_weight: bfloat16 [2, 28, 3584], P('pipe'), may hold values from -0.09375 to 0.09375
- saved_norm: bfloat16 [2, 4, 2048, 3584], P('pipe', 'dp', 'ctx'), may hold values from -6 to 6
- kv_cot: bfloat16 [2, 4, 2048, 512], P('pipe', 'dp', 'ctx'), may hold values from -0.15625 to 0.15625
- gate_cot: bfloat16 [2, 4, 2048, 28], P('pipe', 'dp', 'ctx'), may hold values from -0.15625 to 0.15625
Outputs:
- passed: bfloat16 [2, 4, 2048, 3584], P('pipe', 'dp', 'ctx')
- kv_grad: bfloat16 [2, 3584, 512], P('pipe', ('ctx', 'dp'))
- gate_grad: bfloat16 [2, 28, 3584], P('pipe', None, ('ctx', 'dp'))
Inputs may be any that keep to these rules, and one draw needn't show every extreme that they name: `selected`: for query block b, entry 0 is b; then come min(b, 15) distinct blocks below b in random order, then -1 in the remaining entries.
All inputs are finite; a program needn't handle non-finite values.
Results may differ from a plain program's by a relative error of at most 0.0061.
Values may be sent and summed in bfloat16 or wider, within the bound.
A program may use at most 128 MiB of HBM per device.

v0:
```python
import functools
import math

import jax
import jax.numpy as jnp
from jax import lax
from jax.experimental import pallas as pl
from jax.experimental.pallas import tpu as pltpu
from jax.sharding import PartitionSpec as P


HD = 128
KVH = 2
BLOCK = 64
CHUNKS = 4

epsilon = 1e-06


def passed_along(block, axis, distance):
    devices = range(lax.axis_size(axis))
    route = [((i - distance) % len(devices), i) for i in devices]
    return lax.ppermute(block, axis, route)


def front_kernel(
    ranks, levels, hidden_hbm, gain_ref, gate_ref, weight_ref, saved_hbm, kv_cot_ref, gate_cot_ref,
    normed_hbm, gating_ref, kv_hbm, grads_hbm,
    hidden_ref, normed_ref, saved_ref, full_ref, total_ref, kv_ref, grads_ref,
    load_sem, store_sem, send_sem, recv_sem, kv_send_sem, kv_recv_sem,
):
    pipe = lax.axis_index("pipe")
    mine = lax.axis_index("ctx")
    level = lax.axis_index("dp")
    across = lax.rem(mine + ranks // 2, ranks)
    beside = mine + 1 - 2 * lax.rem(mine, 2)
    corner = lax.rem(beside + ranks // 2, ranks)
    rows = weight_ref.shape[0]
    depth = levels * rows
    length, width = hidden_ref.shape
    tiles = kv_ref.shape[1]
    tile = length // tiles
    heads = gate_ref.shape[0]

    def at(rank, other):
        return (pipe, rank, other)

    loads = [
        pltpu.make_async_copy(hidden_hbm, hidden_ref, load_sem.at[0]),
        pltpu.make_async_copy(saved_hbm, saved_ref, load_sem.at[1]),
        pltpu.make_async_copy(weight_ref, full_ref.at[mine, level], load_sem.at[2]),
    ]
    for load in loads:
        load.start()

    partners = [at(mine, lax.rem(level + d, levels)) for d in range(1, levels)]
    partners += [at(across, level), at(beside, level)]
    barrier = pltpu.get_barrier_semaphore()
    for partner in partners:
        pl.semaphore_signal(
            barrier, inc=1, device_id=partner, device_id_type=pl.DeviceIdType.MESH
        )
    pl.semaphore_wait(barrier, len(partners))

    sent = []

    def send(source, rank, other, target):
        copy = pltpu.make_async_remote_copy(
            src_ref=source,
            dst_ref=full_ref.at[rank, other],
            send_sem=send_sem.at[len(sent)],
            recv_sem=recv_sem.at[rank, other],
            device_id=target,
            device_id_type=pl.DeviceIdType.MESH,
        )
        copy.start()
        sent.append(copy)

    def arrived(rank, other):
        pltpu.make_async_remote_copy(
            src_ref=full_ref.at[rank, other],
            dst_ref=full_ref.at[rank, other],
            send_sem=send_sem.at[0],
            recv_sem=recv_sem.at[rank, other],
            device_id=at(beside, level),
            device_id_type=pl.DeviceIdType.MESH,
        ).wait_recv()

    send(weight_ref, mine, level, at(across, level))
    for d in range(1, levels):
        send(weight_ref, mine, level, at(mine, lax.rem(level + d, levels)))
    send(weight_ref, mine, level, at(beside, level))

    loads[0].wait()

    def norm_tile(i, carry):
        span = pl.ds(pl.multiple_of(i * 64, 64), 64)
        hidden = hidden_ref[span, :].astype(jnp.float32)
        scale = lax.rsqrt(jnp.mean(hidden * hidden, axis=-1, keepdims=True) + epsilon)
        normed_ref[span, :] = (hidden * scale * gain_ref[...]).astype(jnp.bfloat16)
        return carry

    lax.fori_loop(0, length // 64, norm_tile, 0)
    stores = []

    def store(source, target):
        copy = pltpu.make_async_copy(source, target, store_sem.at[len(stores)])
        copy.start()
        stores.append(copy)

    parts = grads_ref.shape[0]
    per_part = grads_ref.shape[1]
    columns = width // parts

    def grad_part(i):
        saved = saved_ref[:, i * columns : (i + 1) * columns]
        kv = lax.dot_general(
            saved, kv_cot_ref[...], (((0,), (0,)), ((), ())), preferred_element_type=jnp.float32
        )
        gate = lax.dot_general(
            gate_cot_ref[...], saved, (((0,), (0,)), ((), ())), preferred_element_type=jnp.float32
        )
        grads_ref[i, :, :rows, :] = kv.reshape(per_part, rows, kv.shape[-1])
        grads_ref[i, :, rows:, :] = jnp.zeros_like(grads_ref[i, :, rows:, :])
        for k in range(per_part):
            grads_ref[i, k, rows : rows + heads, :rows] = gate[:, k * rows : (k + 1) * rows]

    loads[1].wait()
    loads[2].wait()
    for d in range(max(levels, parts)):
        if d < levels - 1:
            other = lax.rem(level + levels - 1 - d, levels)
            arrived(mine, other)
            send(full_ref.at[mine, other], mine, other, at(across, level))
            send(full_ref.at[mine, other], mine, other, at(beside, level))
        if d < levels:
            other = lax.rem(level + levels - d, levels)
            arrived(across, other)
            send(full_ref.at[across, other], across, other, at(beside, level))
        if d < parts:
            grad_part(d)
            if d > 0:
                store(grads_ref.at[d - 1], grads_hbm.at[d - 1])
    store(normed_ref, normed_hbm)

    def term(rank, first, count):
        span = pl.ds(pl.multiple_of(rank * depth, 128), depth)
        return jnp.dot(
            normed_ref[first : first + count, span],
            full_ref[rank].reshape(depth, full_ref.shape[-1]),
            preferred_element_type=jnp.float32,
        )

    total_ref[...] = term(mine, 0, length)
    store(grads_ref.at[parts - 1], grads_hbm.at[parts - 1])
    total_ref[...] += term(across, 0, length)
    for d in range(levels):
        arrived(beside, lax.rem(level + levels - d, levels))
    total_ref[...] += term(beside, 0, length)
    for d in range(levels):
        arrived(corner, lax.rem(level + levels - d, levels))

    kv_sent = []

    def kv_send(rank, t, target):
        copy = pltpu.make_async_remote_copy(
            src_ref=kv_ref.at[rank, t],
            dst_ref=kv_ref.at[rank, t],
            send_sem=kv_send_sem.at[len(kv_sent)],
            recv_sem=kv_recv_sem.at[rank, t],
            device_id=target,
            device_id_type=pl.DeviceIdType.MESH,
        )
        copy.start()
        kv_sent.append(copy)

    def kv_arrived(rank, t):
        pltpu.make_async_remote_copy(
            src_ref=kv_ref.at[rank, t],
            dst_ref=kv_ref.at[rank, t],
            send_sem=kv_send_sem.at[0],
            recv_sem=kv_recv_sem.at[rank, t],
            device_id=at(beside, level),
            device_id_type=pl.DeviceIdType.MESH,
        ).wait_recv()

    def publish(t):
        kv_send(mine, t, at(across, level))
        kv_send(mine, t, at(beside, level))

    for t in range(tiles):
        span = slice(t * tile, (t + 1) * tile)
        projected = total_ref[span, :] + term(corner, t * tile, tile)
        kv_ref[mine, t] = projected.astype(jnp.bfloat16)
        if t > 0:
            publish(t - 1)
    logits = lax.dot_general(
        normed_ref[...], gate_ref[...], (((1,), (1,)), ((), ())),
        preferred_element_type=jnp.float32,
    )
    publish(tiles - 1)
    gating_ref[...] = jax.nn.sigmoid(logits)
    for t in range(tiles):
        kv_arrived(across, t)
        kv_send(across, t, at(beside, level))
    for t in range(tiles):
        kv_arrived(beside, t)
        kv_arrived(corner, t)
    store(kv_ref, kv_hbm)
    for copy in sent + kv_sent:
        copy.wait_send()
    for copy in stores:
        copy.wait()


def front(hidden, gain, gate_rows, weight, saved, kv_cot, gate_cot):
    ranks = lax.axis_size("ctx")
    levels = lax.axis_size("dp")
    length, width = hidden.shape
    heads = gate_rows.shape[0]
    rows, kv_width = weight.shape
    shards = ranks * levels
    parts = ranks
    tiles = 4
    padded = -(-heads // 8) * 8
    low, full = jnp.bfloat16, jnp.float32
    grads_shape = (parts, shards // parts, rows + padded, kv_width)
    kv_shape = (ranks, tiles, length // tiles, kv_width)
    vmem = pl.BlockSpec(memory_space=pltpu.VMEM)
    hbm = pl.BlockSpec(memory_space=pl.ANY)
    normed, gating, kv, grads = pl.pallas_call(
        functools.partial(front_kernel, ranks, levels),
        in_specs=[hbm, vmem, vmem, vmem, hbm, vmem, vmem],
        out_specs=[hbm, vmem, hbm, hbm],
        out_shape=[
            jax.ShapeDtypeStruct((length, width), low),
            jax.ShapeDtypeStruct((length, heads), full),
            jax.ShapeDtypeStruct(kv_shape, low),
            jax.ShapeDtypeStruct(grads_shape, full),
        ],
        scratch_shapes=[
            pltpu.VMEM((length, width), low),
            pltpu.VMEM((length, width), low),
            pltpu.VMEM((length, width), low),
            pltpu.VMEM((ranks, levels, rows, kv_width), low),
            pltpu.VMEM((length, kv_width), full),
            pltpu.VMEM(kv_shape, low),
            pltpu.VMEM(grads_shape, full),
            pltpu.SemaphoreType.DMA((3,)),
            pltpu.SemaphoreType.DMA((parts + 2,)),
            pltpu.SemaphoreType.DMA((4 * levels - 1,)),
            pltpu.SemaphoreType.DMA((ranks, levels)),
            pltpu.SemaphoreType.DMA((3 * tiles,)),
            pltpu.SemaphoreType.DMA((ranks, tiles)),
        ],
        compiler_params=pltpu.CompilerParams(
            collective_id=0, has_side_effects=True, vmem_limit_bytes=48 * 2**20
        ),
    )(hidden, gain, gate_rows, weight, saved, kv_cot, gate_cot)
    return (
        normed,
        gating,
        kv.reshape(ranks * length, kv_width),
        grads.reshape(shards, rows + padded, kv_width),
    )


def attend_kernel(
    first, entries, picks_ref, place_ref, normed_ref, hidden_ref, gating_ref, kv_ref, out_ref,
    picked_ref, values_ref,
):
    step = first + pl.program_id(0)
    place = place_ref[0] + step
    keys = entries * BLOCK
    heads = gating_ref.shape[-1]
    group = heads // KVH
    half = group // 2
    scale = math.log2(math.e) / math.sqrt(HD)
    for c in range(entries):
        chosen = jnp.maximum(picks_ref[step, c], 0)
        tile = kv_ref[pl.ds(pl.multiple_of(chosen * BLOCK, BLOCK), BLOCK), :]
        span = slice(c * BLOCK, (c + 1) * BLOCK)
        for g in range(KVH):
            picked_ref[g, span, :] = tile[:, g * HD : (g + 1) * HD]
            values_ref[g, span, :HD] = tile[:, (KVH + g) * HD : (KVH + g + 1) * HD]
            values_ref[g, span, HD:] = jnp.ones((BLOCK, HD), jnp.bfloat16)
    column = lax.broadcasted_iota(jnp.int32, (BLOCK, keys), 1)
    row = lax.broadcasted_iota(jnp.int32, (BLOCK, keys), 0)
    last = jnp.where(column < BLOCK, row, (place + 1) * BLOCK - 1)
    bias = jnp.where(column <= last, 0.0, -1e30).astype(jnp.float32)
    gating = gating_ref[...]
    for g in range(KVH):
        k_all = picked_ref[g]
        v_all = values_ref[g]
        for part in range(0, group, half):
            first_head = g * group + part
            query = jnp.concatenate(
                [
                    normed_ref[:, (first_head + j) * HD : (first_head + j + 1) * HD]
                    for j in range(half)
                ],
                axis=0,
            )
            scores = lax.dot_general(
                query, k_all, (((1,), (1,)), ((), ())), preferred_element_type=jnp.float32
            )
            scores = (scores.reshape(half, BLOCK, keys) * scale + bias[None]).reshape(
                half * BLOCK, keys
            )
            top = jnp.max(scores, axis=-1, keepdims=True)
            weights = jnp.exp2(scores - top).astype(jnp.bfloat16)
            blended = jnp.dot(weights, v_all, preferred_element_type=jnp.float32)
            attended = blended[:, :HD] / blended[:, HD:]
            for j in range(half):
                h = first_head + j
                span = slice(h * HD, (h + 1) * HD)
                base = hidden_ref[:, span].astype(jnp.float32)
                piece = attended[j * BLOCK : (j + 1) * BLOCK]
                out_ref[:, span] = (base + gating[:, h : h + 1] * piece).astype(jnp.bfloat16)


def attend(first, count, picks, place, normed, hidden, gating, sequence_kv):
    width = normed.shape[1]
    heads = gating.shape[1]
    total, kv_width = sequence_kv.shape
    entries = picks.shape[1]
    return pl.pallas_call(
        functools.partial(attend_kernel, first, entries),
        grid_spec=pltpu.PrefetchScalarGridSpec(
            num_scalar_prefetch=2,
            grid=(count,),
            in_specs=[
                pl.BlockSpec((BLOCK, width), lambda i, *_: (first + i, 0)),
                pl.BlockSpec((BLOCK, width), lambda i, *_: (first + i, 0)),
                pl.BlockSpec((BLOCK, heads), lambda i, *_: (first + i, 0)),
                pl.BlockSpec((total, kv_width), lambda i, *_: (0, 0)),
            ],
            out_specs=pl.BlockSpec((BLOCK, width), lambda i, *_: (i, 0)),
            scratch_shapes=[
                pltpu.VMEM((KVH, entries * BLOCK, HD), jnp.bfloat16),
                pltpu.VMEM((KVH, entries * BLOCK, 2 * HD), jnp.bfloat16),
            ],
        ),
        out_shape=jax.ShapeDtypeStruct((count * BLOCK, width), jnp.bfloat16),
        cost_estimate=pl.CostEstimate(
            flops=6 * count * BLOCK * width * entries * BLOCK,
            bytes_accessed=6 * count * BLOCK * width + 2 * total * kv_width,
            transcendentals=count * BLOCK * heads * entries * BLOCK,
        ),
    )(picks, place, normed, hidden, gating, sequence_kv)


def per_device(
    hidden_in, selected, norm_gain, kv_weight, gate_weight, saved_norm, kv_cot, gate_cot
):
    current = hidden_in[0, 0]
    picks = selected[0, 0]
    length = current.shape[0]
    normed, gating, sequence_kv, grads = front(
        current, norm_gain, gate_weight[0], kv_weight[0], saved_norm[0, 0], kv_cot[0, 0],
        gate_cot[0, 0],
    )
    summed = lax.psum_scatter(grads, ("ctx", "dp"), scatter_dimension=0, tiled=True)[0]
    blocks_here = length // BLOCK
    place = (lax.axis_index("ctx") * blocks_here).astype(jnp.int32)[None]
    chunks = math.gcd(CHUNKS, blocks_here)
    count = blocks_here // chunks
    pieces = []
    for i in range(chunks):
        piece = attend(i * count, count, picks, place, normed, current, gating, sequence_kv)
        pieces.append(passed_along(piece, "pipe", 1))
    passed = jnp.concatenate(pieces, axis=0)[None, None]
    rows = kv_weight.shape[1]
    heads = gate_weight.shape[1]
    kv_grad = summed[None, :rows].astype(jnp.bfloat16)
    gate_grad = summed[None, rows : rows + heads, :rows].astype(jnp.bfloat16)
    return (passed, kv_grad, gate_grad)


def solution(mesh):
    in_specs = (
        P("pipe", "dp", "ctx", None),
        P("pipe", "dp", "ctx", None),
        P("pipe", None),
        P("pipe", ("ctx", "dp"), None),
        P("pipe", None, None),
        P("pipe", "dp", "ctx", None),
        P("pipe", "dp", "ctx", None),
        P("pipe", "dp", "ctx", None),
    )
    out_specs = (
        P("pipe", "dp", "ctx", None),
        P("pipe", ("ctx", "dp"), None),
        P("pipe", None, ("ctx", "dp")),
    )
    return jax.shard_map(
        per_device, mesh=mesh, in_specs=in_specs, out_specs=out_specs, check_vma=False
    )
```

profile of v0, /device:TPU:0, one launch (start us, length us, event | category | flops | bytes accessed | tf_op | source)
XLA Modules:
  0.0 181.2 jit_solution(1878063897760195508)
XLA Ops:
  7.2 0.9 copy.11
  8.1 1.0 copy-done.2
  9.2 0.9 copy-done.3
  10.1 0.9 copy-done.4
  11.0 0.7 copy-done.5
  11.8 48.5 %shard_map.103 = (bf16[512,3584]{1,0:T(8,128)(2,1)}, f32[512,28]{1,0:T(8,128)S(1)}, bf16[4,4,128,512]{3,2,1,0:T(8,128)(2,1)S(1)}, f32[4,4,256,512]{3,2,1,0:T(8,128)}) custom-call(bf16[512,3584]{1,0:T(8,128)(2,1)} %bitcast.24, f32[1,3584]{1,0:T(1,128)S(1)} %copy-done.5, bf16[28,3584]{1,0:T(8,128)(2,1)S(1)} %bitcast.22, bf16[224,512]{1,0:T(8,128)(2,1)S(1)} %bitcast.23, ...), custom_call_target="tpu_custom_call" | custom-call | tf_op jit(solution)/shard_map/pallas_call | solution.py:231
  60.3 1.3 copy-done
  61.6 0.7 copy-done.1
  62.3 10.0 %shard_map.104 = bf16[128,3584]{1,0:T(8,128)(2,1)} custom-call(s32[8,16]{1,0:T(8,128)} %bitcast.31, s32[1]{0:T(128)} %bitcast.1.place_ref, bf16[512,3584]{1,0:T(8,128)(2,1)} %get-tuple-element.7.normed_ref, bf16[512,3584]{1,0:T(8,128)(2,1)} %bitcast.25, f32[512,28]{1,0:T(8,128)} %copy-done.1, bf16[2048,512]{1,0:T(8,128)(2,1)} %bitcast.16), custom_call_target="tpu_custom_call" | custom-call | flops 2818572288 | bytes 4849664 | tf_op jit(solution)/shard_map/pallas_call | solution.py:327
  72.4 1.5 collective-permute-start
  73.9 10.3 %shard_map.105 = bf16[128,3584]{1,0:T(8,128)(2,1)} custom-call(s32[8,16]{1,0:T(8,128)} %bitcast.32, s32[1]{0:T(128)} %bitcast.1.place_ref, bf16[512,3584]{1,0:T(8,128)(2,1)} %get-tuple-element.7.normed_ref, bf16[512,3584]{1,0:T(8,128)(2,1)} %bitcast.26, f32[512,28]{1,0:T(8,128)} %copy-done.1, bf16[2048,512]{1,0:T(8,128)(2,1)} %bitcast.17), custom_call_target="tpu_custom_call" | custom-call | flops 2818572288 | bytes 4849664 | tf_op jit(solution)/shard_map/pallas_call | solution.py:327
  84.2 0.4 collective-permute-start.1
  84.6 10.4 %shard_map.106 = bf16[128,3584]{1,0:T(8,128)(2,1)} custom-call(s32[8,16]{1,0:T(8,128)} %bitcast.33, s32[1]{0:T(128)} %bitcast.1.place_ref, bf16[512,3584]{1,0:T(8,128)(2,1)} %get-tuple-element.7.normed_ref, bf16[512,3584]{1,0:T(8,128)(2,1)} %bitcast.27, f32[512,28]{1,0:T(8,128)} %copy-done.1, bf16[2048,512]{1,0:T(8,128)(2,1)} %bitcast.18), custom_call_target="tpu_custom_call" | custom-call | flops 2818572288 | bytes 4849664 | tf_op jit(solution)/shard_map/pallas_call | solution.py:327
  95.0 1.6 collective-permute-start.2
  96.6 10.4 %shard_map.107 = bf16[128,3584]{1,0:T(8,128)(2,1)} custom-call(s32[8,16]{1,0:T(8,128)} %bitcast.34, s32[1]{0:T(128)} %bitcast.1.place_ref, bf16[512,3584]{1,0:T(8,128)(2,1)} %get-tuple-element.7.normed_ref, bf16[512,3584]{1,0:T(8,128)(2,1)} %bitcast.28, f32[512,28]{1,0:T(8,128)} %copy-done.1, bf16[2048,512]{1,0:T(8,128)(2,1)} %bitcast.19), custom_call_target="tpu_custom_call" | custom-call | flops 2818572288 | bytes 4849664 | tf_op jit(solution)/shard_map/pallas_call | solution.py:327
  107.0 8.5 %collective-permute-done.1 = bf16[128,3584]{1,0:T(8,128)(2,1)S(1)} collective-permute-done((bf16[128,3584]{1,0:T(8,128)(2,1)}, bf16[128,3584]{1,0:T(8,128)(2,1)S(1)}, u32[]{:S(2)}, u32[]{:S(2)}) %collective-permute-start.1) | collective-permute-done | bytes 917536 | tf_op jit(solution)/shard_map/ppermute | solution.py:23
  115.5 19.7 %collective-permute-done.2 = bf16[128,3584]{1,0:T(8,128)(2,1)S(1)} collective-permute-done((bf16[128,3584]{1,0:T(8,128)(2,1)}, bf16[128,3584]{1,0:T(8,128)(2,1)S(1)}, u32[]{:S(2)}, u32[]{:S(2)}) %collective-permute-start.2) | collective-permute-done | bytes 917536 | tf_op jit(solution)/shard_map/ppermute | solution.py:23
  135.1 19.2 %collective-permute-done.3 = bf16[128,3584]{1,0:T(8,128)(2,1)S(1)} collective-permute-done((bf16[128,3584]{1,0:T(8,128)(2,1)}, bf16[128,3584]{1,0:T(8,128)(2,1)S(1)}, u32[]{:S(2)}, u32[]{:S(2)}) %collective-permute-start.3) | collective-permute-done | bytes 917536 | tf_op jit(solution)/shard_map/ppermute | solution.py:23
  154.4 2.0 %maximum_bitcast_fusion = bf16[1,1,512,3584]{3,2,1,0:T(8,128)(2,1)} fusion(bf16[128,3584]{1,0:T(8,128)(2,1)S(1)} %collective-permute-done.3, bf16[128,3584]{1,0:T(8,128)(2,1)S(1)} %collective-permute-done.2, bf16[128,3584]{1,0:T(8,128)(2,1)S(1)} %collective-permute-done.1, bf16[128,3584]{1,0:T(8,128)(2,1)S(1)} %collective-permute-done), kind=kLoop, calls=%fused_computation | loop fusion | flops 14680064 | bytes 7340032 | tf_op jit(solution)/shard_map/broadcast_in_dim | solution.py:372
  156.3 14.6 %reduce-scatter.2.cloned.1.call-done = f32[1,256,512]{2,1,0:T(8,128)} async-done(((f32[16,256,512]{2,1,0:T(8,128)}), f32[1,256,512]{2,1,0:T(8,128)}) %reduce-scatter.2.cloned.1.call-update) | async-done | bytes 524304 | tf_op jit(solution)/shard_map/reduce_scatter | solution.py:363
  170.9 1.1 convert_bitcast_fusion
  172.0 0.6 slice_bitcast_fusion
  172.6 1.1 convert.5
  173.7 0.7 slice.11
  (10 shorter events, 0.1 us)
Async XLA Ops:
  7.2 163.7 %reduce-scatter.2.cloned.1.call-start = ((), (), s32[]{:S(2)}) async-start(), calls=%async_computation.1 | async-start | bytes 8912896 | tf_op jit(solution)/shard_map/reduce_scatter | solution.py:363
  8.1 1.0 copy-start.2
  9.2 0.9 copy-start.3
  10.1 0.9 copy-start.4
  11.0 0.7 copy-start.5
  60.3 1.3 copy-start
  61.6 0.7 copy-start.1
  72.4 34.6 %collective-permute-start = (bf16[128,3584]{1,0:T(8,128)(2,1)}, bf16[128,3584]{1,0:T(8,128)(2,1)S(1)}, u32[]{:S(2)}, u32[]{:S(2)}) collective-permute-start(bf16[128,3584]{1,0:T(8,128)(2,1)} %shard_map.104), channel_id=1, source_target_pairs={{16,0},{0,16},{17,1},{1,17},{18,2},{2,18},{19,3},{3,19},{20,4},{4,... | collective-permute-start | bytes 2752520 | tf_op jit(solution)/shard_map/ppermute | solution.py:23
  84.2 31.3 %collective-permute-start.1 = (bf16[128,3584]{1,0:T(8,128)(2,1)}, bf16[128,3584]{1,0:T(8,128)(2,1)S(1)}, u32[]{:S(2)}, u32[]{:S(2)}) collective-permute-start(bf16[128,3584]{1,0:T(8,128)(2,1)} %shard_map.105), channel_id=1, source_target_pairs={{16,0},{0,16},{17,1},{1,17},{18,2},{2,18},{19,3},{3,19},{20,4},{4,... | collective-permute-start | bytes 2752520 | tf_op jit(solution)/shard_map/ppermute | solution.py:23
  95.0 40.1 %collective-permute-start.2 = (bf16[128,3584]{1,0:T(8,128)(2,1)}, bf16[128,3584]{1,0:T(8,128)(2,1)S(1)}, u32[]{:S(2)}, u32[]{:S(2)}) collective-permute-start(bf16[128,3584]{1,0:T(8,128)(2,1)} %shard_map.106), channel_id=1, source_target_pairs={{16,0},{0,16},{17,1},{1,17},{18,2},{2,18},{19,3},{3,19},{20,4},{4,... | collective-permute-start | bytes 2752520 | tf_op jit(solution)/shard_map/ppermute | solution.py:23
  107.0 47.4 %collective-permute-start.3 = (bf16[128,3584]{1,0:T(8,128)(2,1)}, bf16[128,3584]{1,0:T(8,128)(2,1)S(1)}, u32[]{:S(2)}, u32[]{:S(2)}) collective-permute-start(bf16[128,3584]{1,0:T(8,128)(2,1)} %shard_map.107), channel_id=1, source_target_pairs={{16,0},{0,16},{17,1},{1,17},{18,2},{2,18},{19,3},{3,19},{20,4},{4,... | collective-permute-start | bytes 2752520 | tf_op jit(solution)/shard_map/ppermute | solution.py:23
Sparse Core Ops, SparseCore 0:
  62.5 108.3 reduce-scatter.1
where the time goes:
time: 182 us; the launch traced here: 181 us
  Pallas kernels  89.6 us (49%)
  waiting for transfers between devices  62 us (34%)
  between operations  14.1 us (8%)
  local copies, waits for them, and re-layouts  7.85 us (4%)
  other arithmetic  4.1 us (2%)
  starting transfers between devices  3.61 us (2%)
    pallas_call x1, Pallas kernels, front(): pl.pallas_call(functools.partial(front_kernel, ranks, levels), in_specs=[...  48.5 us
    ppermute x4, waiting for transfers between devices, passed_along(): return lax.ppermute(block, axis, route)  47.4 us
    pallas_call x4, Pallas kernels, attend(): pl.pallas_call(functools.partial(attend_kernel, first, entries), grid_spe...  41.1 us
    reduce_scatter x1, waiting for transfers between devices, per_device(): lax.psum_scatter(grads, ('ctx', 'dp'), scatter_dimension=0, tiled=True)[0]  14.6 us
    unnamed x13, local copies, waits for them, and re-layouts  6.54 us
  transfers between devices with their start and end apart: 5, of which 4 were waited for; matrix products, arithmetic and copies ran while one was open for 1% of the time, Pallas kernels for 23%

commit v1 on v0

--- a/solution.py
+++ b/solution.py
@@ -12,9 +12,15 @@
 HD = 128
 KVH = 2
 BLOCK = 64
-CHUNKS = 4
 
 epsilon = 1e-06
+
+
+def chunk_sizes(blocks):
+    sizes = [1] * min(2, blocks)
+    while sum(sizes) < blocks:
+        sizes.append(min(2, blocks - sum(sizes)))
+    return sizes
 
 
 def passed_along(block, axis, distance):
@@ -24,9 +30,9 @@
 
 
 def front_kernel(
-    ranks, levels, hidden_hbm, gain_ref, gate_ref, weight_ref, saved_hbm, kv_cot_ref, gate_cot_ref,
+    ranks, levels, hidden_hbm, gain_ref, gate_hbm, weight_ref, saved_hbm, kv_cot_hbm, gate_cot_hbm,
     normed_hbm, gating_ref, kv_hbm, grads_hbm,
-    hidden_ref, normed_ref, saved_ref, full_ref, total_ref, kv_ref, grads_ref,
+    gate_ref, kv_cot_ref, gate_cot_ref, hidden_ref, normed_ref, saved_ref, full_ref, total_ref, kv_ref, grads_ref,
     load_sem, store_sem, send_sem, recv_sem, kv_send_sem, kv_recv_sem,
 ):
     pipe = lax.axis_index("pipe")
@@ -49,6 +55,9 @@
         pltpu.make_async_copy(hidden_hbm, hidden_ref, load_sem.at[0]),
         pltpu.make_async_copy(saved_hbm, saved_ref, load_sem.at[1]),
         pltpu.make_async_copy(weight_ref, full_ref.at[mine, level], load_sem.at[2]),
+        pltpu.make_async_copy(kv_cot_hbm, kv_cot_ref, load_sem.at[3]),
+        pltpu.make_async_copy(gate_cot_hbm, gate_cot_ref, load_sem.at[4]),
+        pltpu.make_async_copy(gate_hbm, gate_ref, load_sem.at[5]),
     ]
     for load in loads:
         load.start()
@@ -120,13 +129,16 @@
         gate = lax.dot_general(
             gate_cot_ref[...], saved, (((0,), (0,)), ((), ())), preferred_element_type=jnp.float32
         )
-        grads_ref[i, :, :rows, :] = kv.reshape(per_part, rows, kv.shape[-1])
+        low = grads_ref.dtype
+        grads_ref[i, :, :rows, :] = kv.reshape(per_part, rows, kv.shape[-1]).astype(low)
         grads_ref[i, :, rows:, :] = jnp.zeros_like(grads_ref[i, :, rows:, :])
         for k in range(per_part):
-            grads_ref[i, k, rows : rows + heads, :rows] = gate[:, k * rows : (k + 1) * rows]
-
-    loads[1].wait()
-    loads[2].wait()
+            grads_ref[i, k, rows : rows + heads, :rows] = gate[
+                :, k * rows : (k + 1) * rows
+            ].astype(low)
+
+    for load in loads[1:]:
+        load.wait()
     for d in range(max(levels, parts)):
         if d < levels - 1:
             other = lax.rem(level + levels - 1 - d, levels)
@@ -222,7 +234,7 @@
     shards = ranks * levels
     parts = ranks
     tiles = 4
-    padded = -(-heads // 8) * 8
+    padded = -(-heads // 16) * 16
     low, full = jnp.bfloat16, jnp.float32
     grads_shape = (parts, shards // parts, rows + padded, kv_width)
     kv_shape = (ranks, tiles, length // tiles, kv_width)
@@ -230,23 +242,26 @@
     hbm = pl.BlockSpec(memory_space=pl.ANY)
     normed, gating, kv, grads = pl.pallas_call(
         functools.partial(front_kernel, ranks, levels),
-        in_specs=[hbm, vmem, vmem, vmem, hbm, vmem, vmem],
+        in_specs=[hbm, vmem, hbm, hbm, hbm, hbm, hbm],
         out_specs=[hbm, vmem, hbm, hbm],
         out_shape=[
             jax.ShapeDtypeStruct((length, width), low),
             jax.ShapeDtypeStruct((length, heads), full),
             jax.ShapeDtypeStruct(kv_shape, low),
-            jax.ShapeDtypeStruct(grads_shape, full),
+            jax.ShapeDtypeStruct(grads_shape, low),
         ],
         scratch_shapes=[
+            pltpu.VMEM(gate_rows.shape, low),
+            pltpu.VMEM(kv_cot.shape, low),
+            pltpu.VMEM(gate_cot.shape, low),
             pltpu.VMEM((length, width), low),
             pltpu.VMEM((length, width), low),
             pltpu.VMEM((length, width), low),
             pltpu.VMEM((ranks, levels, rows, kv_width), low),
             pltpu.VMEM((length, kv_width), full),
             pltpu.VMEM(kv_shape, low),
-            pltpu.VMEM(grads_shape, full),
-            pltpu.SemaphoreType.DMA((3,)),
+            pltpu.VMEM(grads_shape, low),
+            pltpu.SemaphoreType.DMA((6,)),
             pltpu.SemaphoreType.DMA((parts + 2,)),
             pltpu.SemaphoreType.DMA((4 * levels - 1,)),
             pltpu.SemaphoreType.DMA((ranks, levels)),
@@ -254,7 +269,7 @@
             pltpu.SemaphoreType.DMA((ranks, tiles)),
         ],
         compiler_params=pltpu.CompilerParams(
-            collective_id=0, has_side_effects=True, vmem_limit_bytes=48 * 2**20
+            collective_id=0, has_side_effects=True, vmem_limit_bytes=60 * 2**20
         ),
     )(hidden, gain, gate_rows, weight, saved, kv_cot, gate_cot)
     return (
@@ -363,12 +378,12 @@
     summed = lax.psum_scatter(grads, ("ctx", "dp"), scatter_dimension=0, tiled=True)[0]
     blocks_here = length // BLOCK
     place = (lax.axis_index("ctx") * blocks_here).astype(jnp.int32)[None]
-    chunks = math.gcd(CHUNKS, blocks_here)
-    count = blocks_here // chunks
     pieces = []
-    for i in range(chunks):
-        piece = attend(i * count, count, picks, place, normed, current, gating, sequence_kv)
+    first = 0
+    for count in chunk_sizes(blocks_here):
+        piece = attend(first, count, picks, place, normed, current, gating, sequence_kv)
         pieces.append(passed_along(piece, "pipe", 1))
+        first += count
     passed = jnp.concatenate(pieces, axis=0)[None, None]
     rows = kv_weight.shape[1]
     heads = gate_weight.shape[1]

time: 182 us -> 162 us (0.89); the launches traced: 181 us -> 159 us
  waiting for transfers between devices: 62 us -> 36.3 us
  other arithmetic: 4.1 us -> 0 us
  Pallas kernels: 89.6 us -> 93.6 us
  starting transfers between devices: 3.61 us -> 5.62 us
    reduce_scatter x1, waiting for transfers between devices: 14.6 us -> 0.01 us  [per_device(): lax.psum_scatter(grads, ('ctx', 'dp'), scatter_dimension=0, tiled=True)[0]]
    ppermute x4 -> x5, waiting for transfers between devices: 47.4 us -> 36.3 us  [passed_along(): return lax.ppermute(block, axis, route)]
    pallas_call x4 -> x5, Pallas kernels: 41.1 us -> 43.1 us  [attend(): pl.pallas_call(functools.partial(attend_kernel, first, entries), grid_spe...]
    ppermute x4 -> x5, starting transfers between devices: 3.57 us -> 5.58 us  [passed_along(): return lax.ppermute(block, axis, route)]
    broadcast_in_dim x1 -> x0, other arithmetic: 1.95 us -> none  [per_device(): passed = jnp.concatenate(pieces, axis=0)[None, None]]
    pallas_call x1, Pallas kernels: 48.5 us -> 50.4 us  [front(): pl.pallas_call(functools.partial(front_kernel, ranks, levels), in_specs=[...]
    unnamed x13 -> x5, local copies, waits for them, and re-layouts: 6.54 us -> 5.1 us
  transfers between devices with their start and end apart: 5 -> 6, of which waited for: 4 -> 2; matrix products, arithmetic and copies ran while one was open for 1% -> 3% of each run, Pallas kernels for 23% -> 27%
where the time goes in v1:
time: 162 us; the launch traced here: 159 us
  Pallas kernels  93.6 us (58%)
  waiting for transfers between devices  36.3 us (22%)
  between operations  14.1 us (9%)
  local copies, waits for them, and re-layouts  9.05 us (6%)
  starting transfers between devices  5.62 us (3%)
    pallas_call x1, Pallas kernels, front(): pl.pallas_call(functools.partial(front_kernel, ranks, levels), in_specs=[...  50.4 us
    pallas_call x5, Pallas kernels, attend(): pl.pallas_call(functools.partial(attend_kernel, first, entries), grid_spe...  43.1 us
    ppermute x5, waiting for transfers between devices, passed_along(): return lax.ppermute(block, axis, route)  36.3 us
    ppermute x5, starting transfers between devices, passed_along(): return lax.ppermute(block, axis, route)  5.58 us
    unnamed x5, local copies, waits for them, and re-layouts  5.1 us
  transfers between devices with their start and end apart: 6, of which 2 were waited for; matrix products, arithmetic and copies ran while one was open for 3% of the time, Pallas kernels for 27%

profile of v1, /device:TPU:0, one launch (start us, length us, event | category | flops | bytes accessed | tf_op | source)
XLA Modules:
  0.0 158.6 jit_solution(2437291082362339125)
XLA Ops:
  7.2 0.0 reduce-scatter.2.cloned.1.call-start
  7.2 1.5 copy.11
  8.8 50.4 %shard_map.103 = (bf16[512,3584]{1,0:T(8,128)(2,1)}, f32[512,28]{1,0:T(8,128)}, bf16[4,4,128,512]{3,2,1,0:T(8,128)(2,1)}, bf16[4,4,256,512]{3,2,1,0:T(8,128)(2,1)}) custom-call(bf16[512,3584]{1,0:T(8,128)(2,1)} %bitcast.14, f32[1,3584]{1,0:T(1,128)} %gain_ref.1, bf16[28,3584]{1,0:T(8,128)(2,1)} %bitcast.30, bf16[224,512]{1,0:T(8,128)(2,1)} %bitcast.31, ...), custom_call_target="tpu_custom_call" | custom-call | tf_op jit(solution)/shard_map/pallas_call | solution.py:243
  59.2 0.0 reduce-scatter.2.cloned.1.call-update
  59.2 6.5 %shard_map.104 = bf16[64,3584]{1,0:T(8,128)(2,1)} custom-call(s32[8,16]{1,0:T(8,128)} %bitcast.32, s32[1]{0:T(128)} %bitcast.1.place_ref, bf16[512,3584]{1,0:T(8,128)(2,1)} %get-tuple-element.7.normed_ref, bf16[512,3584]{1,0:T(8,128)(2,1)} %bitcast.15, f32[512,28]{1,0:T(8,128)} %get-tuple-element.8.gating_ref, bf16[2048,512]{1,0:T(8,128)(2,1)} %bitcast.20), custom_call_target="tpu_custom_call" | custom-call | flops 1409286144 | bytes 3473408 | tf_op jit(solution)/shard_map/pallas_call | solution.py:342
  65.7 1.5 collective-permute-start
  67.3 6.6 %shard_map.105 = bf16[64,3584]{1,0:T(8,128)(2,1)} custom-call(s32[8,16]{1,0:T(8,128)} %bitcast.33, s32[1]{0:T(128)} %bitcast.1.place_ref, bf16[512,3584]{1,0:T(8,128)(2,1)} %get-tuple-element.7.normed_ref, bf16[512,3584]{1,0:T(8,128)(2,1)} %bitcast.16, f32[512,28]{1,0:T(8,128)} %get-tuple-element.8.gating_ref, bf16[2048,512]{1,0:T(8,128)(2,1)} %bitcast.21), custom_call_target="tpu_custom_call" | custom-call | flops 1409286144 | bytes 3473408 | tf_op jit(solution)/shard_map/pallas_call | solution.py:342
  73.8 0.5 collective-permute-start.1
  74.3 10.3 %shard_map.106 = bf16[128,3584]{1,0:T(8,128)(2,1)} custom-call(s32[8,16]{1,0:T(8,128)} %bitcast.34, s32[1]{0:T(128)} %bitcast.1.place_ref, bf16[512,3584]{1,0:T(8,128)(2,1)} %get-tuple-element.7.normed_ref, bf16[512,3584]{1,0:T(8,128)(2,1)} %bitcast.17, f32[512,28]{1,0:T(8,128)} %get-tuple-element.8.gating_ref, bf16[2048,512]{1,0:T(8,128)(2,1)} %bitcast.22), custom_call_target="tpu_custom_call" | custom-call | flops 2818572288 | bytes 4849664 | tf_op jit(solution)/shard_map/pallas_call | solution.py:342
  84.6 1.5 collective-permute-start.2
  86.1 9.9 %shard_map.107 = bf16[128,3584]{1,0:T(8,128)(2,1)} custom-call(s32[8,16]{1,0:T(8,128)} %bitcast.35, s32[1]{0:T(128)} %bitcast.1.place_ref, bf16[512,3584]{1,0:T(8,128)(2,1)} %get-tuple-element.7.normed_ref, bf16[512,3584]{1,0:T(8,128)(2,1)} %bitcast.18, f32[512,28]{1,0:T(8,128)} %get-tuple-element.8.gating_ref, bf16[2048,512]{1,0:T(8,128)(2,1)} %bitcast.23), custom_call_target="tpu_custom_call" | custom-call | flops 2818572288 | bytes 4849664 | tf_op jit(solution)/shard_map/pallas_call | solution.py:342
  96.0 0.5 collective-permute-start.3
  96.5 9.9 %shard_map.108 = bf16[128,3584]{1,0:T(8,128)(2,1)} custom-call(s32[8,16]{1,0:T(8,128)} %bitcast.36, s32[1]{0:T(128)} %bitcast.1.place_ref, bf16[512,3584]{1,0:T(8,128)(2,1)} %get-tuple-element.7.normed_ref, bf16[512,3584]{1,0:T(8,128)(2,1)} %bitcast.19, f32[512,28]{1,0:T(8,128)} %get-tuple-element.8.gating_ref, bf16[2048,512]{1,0:T(8,128)(2,1)} %bitcast.24), custom_call_target="tpu_custom_call" | custom-call | flops 2818572288 | bytes 4849664 | tf_op jit(solution)/shard_map/pallas_call | solution.py:342
  106.4 1.5 collective-permute-start.4
  107.9 0.0 collective-permute-done
  107.9 0.8 constant_dynamic-update-slice_fusion.4
  108.7 0.8 constant_dynamic-update-slice_fusion.3
  109.5 1.0 constant_dynamic-update-slice_fusion.2
  110.5 17.6 %collective-permute-done.3 = bf16[128,3584]{1,0:T(8,128)(2,1)S(1)} collective-permute-done((bf16[128,3584]{1,0:T(8,128)(2,1)}, bf16[128,3584]{1,0:T(8,128)(2,1)S(1)}, u32[]{:S(2)}, u32[]{:S(2)}) %collective-permute-start.3) | collective-permute-done | bytes 917536 | tf_op jit(solution)/shard_map/ppermute | solution.py:29
  128.1 1.0 constant_dynamic-update-slice_fusion.1
  129.1 18.7 %collective-permute-done.4 = bf16[128,3584]{1,0:T(8,128)(2,1)S(1)} collective-permute-done((bf16[128,3584]{1,0:T(8,128)(2,1)}, bf16[128,3584]{1,0:T(8,128)(2,1)S(1)}, u32[]{:S(2)}, u32[]{:S(2)}) %collective-permute-start.4) | collective-permute-done | bytes 917536 | tf_op jit(solution)/shard_map/ppermute | solution.py:29
  147.8 1.0 constant_dynamic-update-slice_fusion
  148.8 1.3 slice_bitcast_fusion
  150.1 1.6 %slice.9 = bf16[1,224,512]{2,1,0:T(8,128)(2,1)} slice(bf16[1,256,512]{2,1,0:T(8,128)(2,1)} %reduce-scatter.2.cloned.1.call-done), slice={[0:1], [0:224], [0:512]} | slice | bytes 458752 | tf_op jit(solution)/shard_map/slice | solution.py:390
  (3 shorter events, 0.0 us)
Async XLA Ops:
  7.2 141.6 %reduce-scatter.2.cloned.1.call-start = ((), (), s32[]{:S(2)}) async-start(), calls=%async_computation.1 | async-start | bytes 4456448 | tf_op jit(solution)/shard_map/reduce_scatter | solution.py:378
  65.7 42.2 %collective-permute-start = (bf16[64,3584]{1,0:T(8,128)(2,1)}, bf16[64,3584]{1,0:T(8,128)(2,1)S(1)}, u32[]{:S(2)}, u32[]{:S(2)}) collective-permute-start(bf16[64,3584]{1,0:T(8,128)(2,1)} %shard_map.104), channel_id=1, source_target_pairs={{16,0},{0,16},{17,1},{1,17},{18,2},{2,18},{19,3},{3,19},{20,4},{4,... | collective-permute-start | bytes 1376264 | tf_op jit(solution)/shard_map/ppermute | solution.py:29
  73.8 34.9 %collective-permute-start.1 = (bf16[64,3584]{1,0:T(8,128)(2,1)}, bf16[64,3584]{1,0:T(8,128)(2,1)S(1)}, u32[]{:S(2)}, u32[]{:S(2)}) collective-permute-start(bf16[64,3584]{1,0:T(8,128)(2,1)} %shard_map.105), channel_id=1, source_target_pairs={{16,0},{0,16},{17,1},{1,17},{18,2},{2,18},{19,3},{3,19},{20,4},{4,... | collective-permute-start | bytes 1376264 | tf_op jit(solution)/shard_map/ppermute | solution.py:29
  84.6 24.9 %collective-permute-start.2 = (bf16[128,3584]{1,0:T(8,128)(2,1)}, bf16[128,3584]{1,0:T(8,128)(2,1)S(1)}, u32[]{:S(2)}, u32[]{:S(2)}) collective-permute-start(bf16[128,3584]{1,0:T(8,128)(2,1)} %shard_map.106), channel_id=1, source_target_pairs={{16,0},{0,16},{17,1},{1,17},{18,2},{2,18},{19,3},{3,19},{20,4},{4,... | collective-permute-start | bytes 2752520 | tf_op jit(solution)/shard_map/ppermute | solution.py:29
  96.0 32.1 %collective-permute-start.3 = (bf16[128,3584]{1,0:T(8,128)(2,1)}, bf16[128,3584]{1,0:T(8,128)(2,1)S(1)}, u32[]{:S(2)}, u32[]{:S(2)}) collective-permute-start(bf16[128,3584]{1,0:T(8,128)(2,1)} %shard_map.107), channel_id=1, source_target_pairs={{16,0},{0,16},{17,1},{1,17},{18,2},{2,18},{19,3},{3,19},{20,4},{4,... | collective-permute-start | bytes 2752520 | tf_op jit(solution)/shard_map/ppermute | solution.py:29
  106.4 41.4 %collective-permute-start.4 = (bf16[128,3584]{1,0:T(8,128)(2,1)}, bf16[128,3584]{1,0:T(8,128)(2,1)S(1)}, u32[]{:S(2)}, u32[]{:S(2)}) collective-permute-start(bf16[128,3584]{1,0:T(8,128)(2,1)} %shard_map.108), channel_id=1, source_target_pairs={{16,0},{0,16},{17,1},{1,17},{18,2},{2,18},{19,3},{3,19},{20,4},{4,... | collective-permute-start | bytes 2752520 | tf_op jit(solution)/shard_map/ppermute | solution.py:29
Sparse Core Ops, SparseCore 0:
  59.3 78.4 reduce-scatter.1
